TPU v7x, 128 devices: a whole 4x4x4 slice. The times are simulated.
128 devices in a mesh: fsdp: 4 (over z), tp: 32 (over y, x, core).
Axes of the slice: x: 4, y: 4, z: 4, core: 2. Of those that a mesh axis runs over, the one named last changes fastest.
Arguments:
- inputs: bfloat16 [2048, 4096], P('fsdp'), may hold values from -6 to 6
- out_grad: bfloat16 [2048, 4096], P('fsdp'), may hold values from -6 to 6
- gate_tiles: bfloat16 [32, 16, 128, 128], P('tp', 'fsdp'), may hold values from -0.25 to 0.25
- up_tiles: bfloat16 [32, 16, 128, 128], P('tp', 'fsdp'), may hold values from -0.25 to 0.25
- down_tiles: bfloat16 [32, 16, 128, 128], P('tp', 'fsdp'), may hold values from -0.125 to 0.125
- in_rows: int32 [32, 16], P('tp'), may hold values from 0 to 31, as said below
- in_cols: int32 [32, 16], P('tp'), may hold values from 0 to 3
- down_rows: int32 [32, 16], P('tp'), may hold values from 0 to 3, as said below
- down_cols: int32 [32, 16], P('tp'), may hold values from 0 to 31
Outputs:
- ffn_out: bfloat16 [2048, 4096], P('fsdp', 'tp')
- input_grad: bfloat16 [2048, 4096], P('fsdp', 'tp')
- gate_grad: float32 [32, 16, 128, 128], P('tp', 'fsdp')
- up_grad: float32 [32, 16, 128, 128], P('tp', 'fsdp')
- down_grad: float32 [32, 16, 128, 128], P('tp', 'fsdp')
Inputs may be any that keep to these rules, and one draw needn't show every extreme that they name: For each index of the first dimension, the pairs (in_rows, in_cols) are distinct. For each index of the first dimension, the pairs (down_rows, down_cols) are distinct.
All inputs are finite; a program needn't handle non-finite values.
Results may differ from a plain program's by a relative error of at most 0.014.
Values may be sent and summed in bfloat16 or wider, within the bound.
A program may use at most 128 MiB of HBM per device.

v0:
```python
import functools

import jax
import jax.numpy as jnp
from jax import lax
from jax.experimental import pallas as pl
from jax.experimental.pallas import tpu as pltpu
from jax.sharding import PartitionSpec as P

RING = 4
CHUNKS = 2
F32 = jnp.float32
BF16 = jnp.bfloat16
NT = (((1,), (1,)), ((), ()))
TN = (((0,), (0,)), ((), ()))


def up32(ref, *idx):
    return ref[idx].astype(F32)


def kernel(
    x_hbm, og_hbm, gt_hbm, ut_hbm, dt_hbm, rows_in, cols_in, rows_dn, cols_dn, inv,
    ffn_ref, ing_ref, gg_ref, ug_ref, dg_ref,
    x, og, tg, tu, td, wgu, wd, hid, act, gb, part, rc, r1r, r1f, q2, r2r, r2f, gr, rzr, rzf,
    lsem, ags, agr, cs, cr, s1s, s1r, s2s, s2r, zs, zr,
):
    z = lax.axis_index("fsdp")
    t = lax.axis_index("tp")
    core = lax.rem(t, 2)
    chip = t // 2
    px = lax.rem(chip, RING)
    py = chip // RING
    tok = x.shape[1]
    blk = tg.shape[1]
    n_tiles = tg.shape[0] - 1
    row_blocks = x.shape[0]
    col_blocks = wd.shape[0] // blk
    per = n_tiles // RING
    ct = tok // CHUNKS
    ht = ct // 4

    def wrap(v):
        return lax.rem(v + RING, RING)

    def dev(zz, yy, xx, cc):
        return (zz, (yy * RING + xx) * 2 + cc)

    def nbr(axis, step):
        if axis == "x":
            return dev(z, py, wrap(px + step), core)
        if axis == "y":
            return dev(z, wrap(py + step), px, core)
        return dev(wrap(z + step), py, px, core)

    partner = dev(z, py, px, 1 - core)
    pos = {"x": px, "y": py, "z": z}
    axes = (("x", "y"), ("y", "x"))

    def remote(src, dst, ss, rs, to):
        return pltpu.make_async_remote_copy(
            src_ref=src, dst_ref=dst, send_sem=ss, recv_sem=rs,
            device_id=to, device_id_type=pl.DeviceIdType.MESH,
        )

    sends = []

    def send(src, dst, ss, rs, to):
        c = remote(src, dst, ss, rs, to)
        c.start()
        sends.append(c)

    tiles_hbm = (gt_hbm, ut_hbm, dt_hbm)
    tiles = (tg, tu, td)
    own = pl.ds(z * per, per)
    loads = [
        pltpu.make_async_copy(tiles_hbm[m].at[0], tiles[m].at[own], lsem.at[m]) for m in range(3)
    ]
    for c in loads:
        c.start()

    def load_block(r, carry):
        cols = pl.ds(r * blk, blk)
        pltpu.make_async_copy(x_hbm.at[:, cols], x.at[r], lsem.at[3]).start()
        pltpu.make_async_copy(og_hbm.at[:, cols], og.at[r], lsem.at[4]).start()
        return carry

    lax.fori_loop(0, row_blocks, load_block, 0)

    barrier = pltpu.get_barrier_semaphore()
    everyone = [partner] + [nbr(a, s) for a in "xyz" for s in (1, -1)]
    for to in everyone:
        pl.semaphore_signal(barrier, inc=1, device_id=to, device_id_type=pl.DeviceIdType.MESH)
    pl.semaphore_wait(barrier, len(everyone))

    def ag_own(m):
        for d, step in enumerate((1, -1)):
            send(tiles_hbm[m].at[0], tiles[m].at[own], ags.at[m, d], agr.at[m, d], nbr("z", step))

    def ag_wait(m, d):
        slot = tiles[m].at[pl.ds(wrap(z - 1 if d == 0 else z + 1) * per, per)]
        remote(slot, slot, ags.at[m, d], agr.at[m, d], partner).wait_recv()

    half = per // 2

    def ag_relay(m):
        for d, step in enumerate((1, -1)):
            ag_wait(m, d)
            piece = tiles[m].at[pl.ds(wrap(z - step) * per + d * half, half)]
            send(piece, piece, ags.at[m, 2 + d], agr.at[m, 2 + d], nbr("z", step))

    def ag_last(m):
        for d in range(2):
            piece = tiles[m].at[pl.ds(wrap(z + 2) * per + d * half, half)]
            remote(piece, piece, ags.at[m, 2 + d], agr.at[m, 2 + d], partner).wait_recv()

    ag_own(0)
    ag_own(1)

    for m in range(3):
        tiles[m][n_tiles] = jnp.zeros((blk, blk), BF16)

    ag_relay(0)
    ag_relay(1)
    ag_own(2)
    loads[0].wait()
    loads[1].wait()
    ag_last(0)
    ag_last(1)

    def build_gu(r, carry):
        rows = pl.ds(r * blk, blk)
        for c in range(col_blocks):
            i = inv[0, r * col_blocks + c]
            wgu[rows, 2 * c * blk:(2 * c + 1) * blk] = tg[i]
            wgu[rows, (2 * c + 1) * blk:(2 * c + 2) * blk] = tu[i]
        return carry

    lax.fori_loop(0, row_blocks, build_gu, 0)
    ag_relay(2)
    pltpu.make_async_copy(x, x, lsem.at[3]).wait()

    def wide(ref, rows):
        return jnp.concatenate([ref[r, rows] for r in range(ref.shape[0])], axis=1)

    def forward(n, carry):
        rows = pl.ds((n // col_blocks) * ct, ct)
        c = lax.rem(n, col_blocks)
        cols = pl.ds(c * 2 * blk, 2 * blk)
        h = jnp.dot(wide(x, rows), wgu[:, cols], preferred_element_type=F32)
        hid[rows, cols] = h
        gate = h[:, :blk]
        act[c, rows] = (gate * jax.nn.sigmoid(gate) * h[:, blk:]).astype(BF16)
        return carry

    lax.fori_loop(0, CHUNKS * col_blocks, forward, 0)
    loads[2].wait()
    pltpu.make_async_copy(og, og, lsem.at[4]).wait()
    ag_last(2)

    def build_dn(j, carry):
        cols = pl.ds(j * blk, blk)
        for c in range(col_blocks):
            wd[c * blk:(c + 1) * blk, cols] = td[inv[1, c * row_blocks + j]]
        return carry

    lax.fori_loop(0, row_blocks, build_dn, 0)

    def put(i, n, val):
        yy = n // RING
        xx = lax.rem(n, RING)
        for cc in range(2):
            for a, (d1, d2) in enumerate(((xx, yy), (yy, xx))):
                for h in range(2):
                    r0 = (a * 2 + h) * ht
                    part[i, cc, a, d1, h, d2] = val[r0:r0 + ht, cc * blk:(cc + 1) * blk].astype(BF16)

    def out_part(k):
        def step(n, carry):
            val = jnp.dot(
                wide(act, pl.ds(k * ct, ct)), wd[:, pl.ds(n * 2 * blk, 2 * blk)],
                preferred_element_type=F32,
            )
            put(k, n, val)
            return carry

        lax.fori_loop(0, row_blocks // 2, step, 0)

    def in_part(k):
        def step(n, carry):
            val = lax.dot_general(
                wide(gb, pl.ds(k * ct, ct)), wgu[pl.ds(n * 2 * blk, 2 * blk), :], NT,
                preferred_element_type=F32,
            )
            put(CHUNKS + k, n, val)
            return carry

        lax.fori_loop(0, row_blocks // 2, step, 0)

    def core_send(i):
        for a in range(2):
            send(part.at[i, 1 - core, a], rc.at[i, a], cs.at[i, a], cr.at[i, a], partner)

    def recv(ref, ss, rs):
        remote(ref, ref, ss, rs, partner).wait_recv()

    def ev_a(i):
        for a in range(2):
            ax = axes[a][0]
            p = pos[ax]
            e = i * 2 + a
            recv(rc.at[i, a], cs.at[i, a], cr.at[i, a])
            far = wrap(p + 2)
            part[i, core, a, far] = (up32(part, i, core, a, far) + up32(rc, i, a, far)).astype(BF16)
            for d, s in enumerate((1, -1)):
                send(part.at[i, core, a, far, d], r1r.at[e, d], s1s.at[e, d], s1r.at[e, d], nbr(ax, s))
            for d, s in enumerate((1, -1)):
                q = wrap(p + s)
                h = 1 - d
                part[i, core, a, q, h] = (
                    up32(part, i, core, a, q, h) + up32(rc, i, a, q, h)
                ).astype(BF16)
                send(
                    part.at[i, core, a, q, h], r1f.at[e, d, h], s1s.at[e, 2 + d],
                    s1r.at[e, 2 + d], nbr(ax, s),
                )

    def ev_b(i):
        for a in range(2):
            ax = axes[a][0]
            p = pos[ax]
            e = i * 2 + a
            for d, s in enumerate((1, -1)):
                q = wrap(p + s)
                recv(r1r.at[e, d], s1s.at[e, d], s1r.at[e, d])
                part[i, core, a, q, d] = (
                    up32(part, i, core, a, q, d) + up32(rc, i, a, q, d) + up32(r1r, e, d)
                ).astype(BF16)
                send(
                    part.at[i, core, a, q, d], r1f.at[e, d, d], s1s.at[e, 4 + d],
                    s1r.at[e, 4 + d], nbr(ax, s),
                )

    def ev_c(i):
        for a in range(2):
            ax, ax2 = axes[a]
            p = pos[ax]
            q = pos[ax2]
            e = i * 2 + a
            for d in range(2):
                recv(r1f.at[e, d, 1 - d], s1s.at[e, 2 + d], s1r.at[e, 2 + d])
                recv(r1f.at[e, d, d], s1s.at[e, 4 + d], s1r.at[e, 4 + d])
            for h in range(2):
                val = (
                    up32(part, i, core, a, p, h) + up32(rc, i, a, p, h)
                    + up32(r1f, e, 0, h) + up32(r1f, e, 1, h)
                ).astype(BF16)
                for d2 in range(RING):
                    q2[e, d2, h] = val[d2]
            far = wrap(q + 2)
            for d, s in enumerate((1, -1)):
                send(q2.at[e, far, d], r2r.at[e, d], s2s.at[e, d], s2r.at[e, d], nbr(ax2, s))
            for d, s in enumerate((1, -1)):
                send(
                    q2.at[e, wrap(q + s), 1 - d], r2f.at[e, d, 1 - d], s2s.at[e, 2 + d],
                    s2r.at[e, 2 + d], nbr(ax2, s),
                )

    def ev_d(i):
        for a in range(2):
            ax2 = axes[a][1]
            q = pos[ax2]
            e = i * 2 + a
            for d, s in enumerate((1, -1)):
                w = wrap(q + s)
                recv(r2r.at[e, d], s2s.at[e, d], s2r.at[e, d])
                q2[e, w, d] = (up32(q2, e, w, d) + up32(r2r, e, d)).astype(BF16)
                send(
                    q2.at[e, w, d], r2f.at[e, d, d], s2s.at[e, 4 + d], s2r.at[e, 4 + d],
                    nbr(ax2, s),
                )

    def ev_e(i):
        out = ffn_ref if i < CHUNKS else ing_ref
        for a in range(2):
            q = pos[axes[a][1]]
            e = i * 2 + a
            for d in range(2):
                recv(r2f.at[e, d, 1 - d], s2s.at[e, 2 + d], s2r.at[e, 2 + d])
                recv(r2f.at[e, d, d], s2s.at[e, 4 + d], s2r.at[e, 4 + d])
            for h in range(2):
                r0 = (i % CHUNKS) * ct + (a * 2 + h) * ht
                out[r0:r0 + ht, :] = (
                    up32(q2, e, q, h) + up32(r2f, e, 0, h) + up32(r2f, e, 1, h)
                ).astype(BF16)

    def ev_z0():
        far = wrap(z + 2)
        for d, s in enumerate((1, -1)):
            send(gr.at[far, d], rzr.at[d], zs.at[d], zr.at[d], nbr("z", s))
        for d, s in enumerate((1, -1)):
            send(gr.at[wrap(z + s), 1 - d], rzf.at[d, 1 - d], zs.at[2 + d], zr.at[2 + d], nbr("z", s))

    def ev_z1():
        for d, s in enumerate((1, -1)):
            q = wrap(z + s)
            recv(rzr.at[d], zs.at[d], zr.at[d])
            gr[q, d] = (up32(gr, q, d) + up32(rzr, d)).astype(BF16)
            send(gr.at[q, d], rzf.at[d, d], zs.at[4 + d], zr.at[4 + d], nbr("z", s))

    def ev_z2():
        for d in range(2):
            recv(rzf.at[d, 1 - d], zs.at[2 + d], zr.at[2 + d])
            recv(rzf.at[d, d], zs.at[4 + d], zr.at[4 + d])
        for h in range(2):
            for m, out in enumerate((gg_ref, ug_ref, dg_ref)):
                for e in range(half):
                    out[0, h * half + e] = (
                        up32(gr, z, h, m, e) + up32(rzf, 0, h, m, e) + up32(rzf, 1, h, m, e)
                    )

    def back(k):
        rows = pl.ds(k * ct, ct)

        def step(n, carry):
            ag = lax.dot_general(
                wide(og, rows), wd[pl.ds(n * 2 * blk, 2 * blk), :], NT, preferred_element_type=F32
            )
            for e in range(2):
                c = n * 2 + e
                c0 = c * 2 * blk
                gate = hid[rows, pl.ds(c0, blk)]
                up = hid[rows, pl.ds(c0 + blk, blk)]
                a = ag[:, e * blk:(e + 1) * blk]
                s = jax.nn.sigmoid(gate)
                gb[c, rows, :blk] = (a * up * s * (1.0 + gate * (1.0 - s))).astype(BF16)
                gb[c, rows, blk:] = (a * (gate * s)).astype(BF16)
            return carry

        lax.fori_loop(0, col_blocks // 2, step, 0)

    def grads():
        def step(k, carry):
            d = k // per
            e = lax.rem(k, per)
            h = e // half
            e = lax.rem(e, half)
            xk = x[rows_in[0, k]]
            bk = gb[cols_in[0, k]]
            g = lax.dot_general(xk, bk, TN, preferred_element_type=F32).astype(BF16)
            gr[d, h, 0, e] = g[:, :blk]
            gr[d, h, 1, e] = g[:, blk:]
            ak = act[rows_dn[0, k]]
            ok = og[cols_dn[0, k]]
            gr[d, h, 2, e] = lax.dot_general(ak, ok, TN, preferred_element_type=F32).astype(BF16)
            return carry

        lax.fori_loop(0, n_tiles, step, 0)

    out_part(0)
    core_send(0)
    out_part(1)
    core_send(1)
    ev_a(0)
    back(0)
    ev_a(1)
    ev_b(0)
    back(1)
    ev_b(1)
    in_part(0)
    core_send(2)
    ev_c(0)
    in_part(1)
    core_send(3)
    ev_a(2)
    ev_c(1)
    ev_d(0)
    grads()
    ev_z0()
    ev_a(3)
    ev_b(2)
    ev_e(0)
    ev_d(1)
    ev_b(3)
    ev_c(2)
    ev_z1()
    ev_e(1)
    ev_c(3)
    ev_d(2)
    ev_d(3)
    ev_e(2)
    ev_z2()
    ev_e(3)
    for c in sends:
        c.wait_send()


def on_device(
    inputs, out_grad, gate_tiles, up_tiles, down_tiles, in_rows, in_cols, down_rows, down_cols
):
    tok, width = inputs.shape
    blk = gate_tiles.shape[2]
    n_tiles = in_rows.shape[1]
    row_blocks = width // blk
    hidden = n_tiles * blk // 4
    steps = 2 * CHUNKS
    ht = tok // (CHUNKS * 4)
    half = n_tiles // RING // 2
    ev = steps * 2
    any_spec = pl.BlockSpec(memory_space=pl.ANY)
    smem = pl.BlockSpec(memory_space=pltpu.SMEM)
    vmem = pl.BlockSpec(memory_space=pltpu.VMEM)
    dma = pltpu.SemaphoreType.DMA
    col_blocks = hidden // blk
    keys = jnp.concatenate(
        [in_rows * col_blocks + in_cols, down_rows * row_blocks + down_cols], axis=0
    )
    cells = jnp.arange(row_blocks * col_blocks, dtype=jnp.int32)
    order = jnp.arange(n_tiles, dtype=jnp.int32)
    inv = n_tiles + jnp.sum(
        jnp.where(keys[:, :, None] == cells, order[:, None] - n_tiles, 0), axis=1, dtype=jnp.int32
    )
    return pl.pallas_call(
        kernel,
        out_shape=(
            jax.ShapeDtypeStruct((tok, blk), BF16),
            jax.ShapeDtypeStruct((tok, blk), BF16),
            jax.ShapeDtypeStruct(gate_tiles.shape, F32),
            jax.ShapeDtypeStruct(gate_tiles.shape, F32),
            jax.ShapeDtypeStruct(gate_tiles.shape, F32),
        ),
        in_specs=[any_spec] * 5 + [smem] * 5,
        out_specs=[vmem] * 5,
        scratch_shapes=[
            pltpu.VMEM((row_blocks, tok, blk), BF16),
            pltpu.VMEM((row_blocks, tok, blk), BF16),
            pltpu.VMEM((n_tiles + 1, blk, blk), BF16),
            pltpu.VMEM((n_tiles + 1, blk, blk), BF16),
            pltpu.VMEM((n_tiles + 1, blk, blk), BF16),
            pltpu.VMEM((width, 2 * hidden), BF16),
            pltpu.VMEM((hidden, width), BF16),
            pltpu.VMEM((tok, 2 * hidden), F32),
            pltpu.VMEM((hidden // blk, tok, blk), BF16),
            pltpu.VMEM((hidden // blk, tok, 2 * blk), BF16),
            pltpu.VMEM((steps, 2, 2, RING, 2, RING, ht, blk), BF16),
            pltpu.VMEM((steps, 2, RING, 2, RING, ht, blk), BF16),
            pltpu.VMEM((ev, 2, RING, ht, blk), BF16),
            pltpu.VMEM((ev, 2, 2, RING, ht, blk), BF16),
            pltpu.VMEM((ev, RING, 2, ht, blk), BF16),
            pltpu.VMEM((ev, 2, ht, blk), BF16),
            pltpu.VMEM((ev, 2, 2, ht, blk), BF16),
            pltpu.VMEM((RING, 2, 3, half, blk, blk), BF16),
            pltpu.VMEM((2, 3, half, blk, blk), BF16),
            pltpu.VMEM((2, 2, 3, half, blk, blk), BF16),
            dma((5,)),
            dma((3, 4)),
            dma((3, 4)),
            dma((steps, 2)),
            dma((steps, 2)),
            dma((ev, 6)),
            dma((ev, 6)),
            dma((ev, 6)),
            dma((ev, 6)),
            dma((6,)),
            dma((6,)),
        ],
        compiler_params=pltpu.CompilerParams(
            collective_id=0, has_side_effects=True, vmem_limit_bytes=60 * 1024 * 1024
        ),
    )(inputs, out_grad, gate_tiles, up_tiles, down_tiles, in_rows, in_cols, down_rows, down_cols,
      inv)


def solution(mesh):
    in_specs = (
        P("fsdp", None),
        P("fsdp", None),
        P("tp", "fsdp", None, None),
        P("tp", "fsdp", None, None),
        P("tp", "fsdp", None, None),
        P("tp", None),
        P("tp", None),
        P("tp", None),
        P("tp", None),
    )
    out_specs = (
        P("fsdp", "tp"),
        P("fsdp", "tp"),
        P("tp", "fsdp", None, None),
        P("tp", "fsdp", None, None),
        P("tp", "fsdp", None, None),
    )
    return jax.shard_map(
        on_device, mesh=mesh, in_specs=in_specs, out_specs=out_specs, check_vma=False
    )
```

profile of v0, /device:TPU:0, one launch (start us, length us, event | category | flops | bytes accessed | tf_op | source)
XLA Modules:
  0.0 89.6 jit_solution(11251396998373403512)
XLA Ops:
  0.6 0.7 multiply_add_fusion
  1.4 0.1 select_reduce_fusion
  1.5 0.6 broadcast_add_fusion.inv
  2.0 79.4 %shard_map.128 = (bf16[512,128]{1,0:T(8,128)(2,1)}, bf16[512,128]{1,0:T(8,128)(2,1)}, f32[1,4,128,128]{3,2,1,0:T(8,128)}, f32[1,4,128,128]{3,2,1,0:T(8,128)}, f32[1,4,128,128]{3,2,1,0:T(8,128)}) custom-call(bf16[512,4096]{1,0:T(8,128)(2,1)} %x_hbm.1, bf16[512,4096]{1,0:T(8,128)(2,1)} %og_hbm.1, bf16[1,4,128,128]{3,2,1,0:T(8,128)(2,1)} %gt_hbm.1, ...), custom_call_target="tpu_custom_call" | custom-call | tf_op jit(solution)/shard_map/pallas_call | solution.py:423
  81.5 1.6 %copy.19 = bf16[512,128]{1,0:T(8,128)(2,1)} copy(bf16[512,128]{1,0:T(8,128)(2,1)} %get-tuple-element.12) | data formatting | bytes 262144
  83.0 1.6 %copy.20 = bf16[512,128]{1,0:T(8,128)(2,1)} copy(bf16[512,128]{1,0:T(8,128)(2,1)} %get-tuple-element.13) | data formatting | bytes 262144
  84.6 1.7 %copy.21 = f32[1,4,128,128]{3,2,1,0:T(8,128)} copy(f32[1,4,128,128]{3,2,1,0:T(8,128)} %get-tuple-element.14) | data formatting | bytes 524288
  86.3 1.7 %copy.22 = f32[1,4,128,128]{3,2,1,0:T(8,128)} copy(f32[1,4,128,128]{3,2,1,0:T(8,128)} %get-tuple-element.15) | data formatting | bytes 524288
  87.9 1.7 %copy.23 = f32[1,4,128,128]{3,2,1,0:T(8,128)} copy(f32[1,4,128,128]{3,2,1,0:T(8,128)} %get-tuple-element.16) | data formatting | bytes 524288
  (2 shorter events, 0.0 us)
where the time goes:
time: 90.5 us; the launch traced here: 89.6 us
  Pallas kernels  79.4 us (88%)
  local copies, waits for them, and re-layouts  8.14 us (9%)
  other arithmetic  1.38 us (2%)
    pallas_call x1, Pallas kernels, on_device(): pl.pallas_call(kernel, out_shape=(jax.ShapeDtypeStruct((tok, blk), BF16),...  79.4 us
    unnamed x5, local copies, waits for them, and re-layouts  8.14 us

commit v1 on v0

--- a/solution.py
+++ b/solution.py
@@ -20,9 +20,10 @@
 
 
 def kernel(
-    x_hbm, og_hbm, gt_hbm, ut_hbm, dt_hbm, rows_in, cols_in, rows_dn, cols_dn, inv,
-    ffn_ref, ing_ref, gg_ref, ug_ref, dg_ref,
+    x_hbm, og_hbm, gt_hbm, ut_hbm, dt_hbm, rows_in_hbm, cols_in_hbm, rows_dn_hbm, cols_dn_hbm,
+    out_ref, grad_ref,
     x, og, tg, tu, td, wgu, wd, hid, act, gb, part, rc, r1r, r1f, q2, r2r, r2f, gr, rzr, rzf,
+    lists, inv_in, inv_dn,
     lsem, ags, agr, cs, cr, s1s, s1r, s2s, s2r, zs, zr,
 ):
     z = lax.axis_index("fsdp")
@@ -87,6 +88,13 @@
 
     lax.fori_loop(0, row_blocks, load_block, 0)
 
+    lists_hbm = (rows_in_hbm, cols_in_hbm, rows_dn_hbm, cols_dn_hbm)
+    list_loads = [
+        pltpu.make_async_copy(lists_hbm[j].at[0], lists.at[j], lsem.at[5 + j]) for j in range(4)
+    ]
+    for c in list_loads:
+        c.start()
+
     barrier = pltpu.get_barrier_semaphore()
     everyone = [partner] + [nbr(a, s) for a in "xyz" for s in (1, -1)]
     for to in everyone:
@@ -117,6 +125,22 @@
     ag_own(0)
     ag_own(1)
 
+    for c in list_loads:
+        c.wait()
+    keys_in = [lists[0, k] * col_blocks + lists[1, k] for k in range(n_tiles)]
+    keys_dn = [lists[2, k] * row_blocks + lists[3, k] for k in range(n_tiles)]
+
+    def table(i, carry):
+        v = jnp.int32(n_tiles)
+        w = jnp.int32(n_tiles)
+        for k in range(n_tiles):
+            v = jnp.where(keys_in[k] == i, jnp.int32(k), v)
+            w = jnp.where(keys_dn[k] == i, jnp.int32(k), w)
+        inv_in[i] = v
+        inv_dn[i] = w
+        return carry
+
+    lax.fori_loop(0, row_blocks * col_blocks, table, 0)
     for m in range(3):
         tiles[m][n_tiles] = jnp.zeros((blk, blk), BF16)
 
@@ -131,7 +155,7 @@
     def build_gu(r, carry):
         rows = pl.ds(r * blk, blk)
         for c in range(col_blocks):
-            i = inv[0, r * col_blocks + c]
+            i = inv_in[r * col_blocks + c]
             wgu[rows, 2 * c * blk:(2 * c + 1) * blk] = tg[i]
             wgu[rows, (2 * c + 1) * blk:(2 * c + 2) * blk] = tu[i]
         return carry
@@ -161,7 +185,7 @@
     def build_dn(j, carry):
         cols = pl.ds(j * blk, blk)
         for c in range(col_blocks):
-            wd[c * blk:(c + 1) * blk, cols] = td[inv[1, c * row_blocks + j]]
+            wd[c * blk:(c + 1) * blk, cols] = td[inv_dn[c * row_blocks + j]]
         return carry
 
     lax.fori_loop(0, row_blocks, build_dn, 0)
@@ -281,7 +305,6 @@
                 )
 
     def ev_e(i):
-        out = ffn_ref if i < CHUNKS else ing_ref
         for a in range(2):
             q = pos[axes[a][1]]
             e = i * 2 + a
@@ -290,7 +313,7 @@
                 recv(r2f.at[e, d, d], s2s.at[e, 4 + d], s2r.at[e, 4 + d])
             for h in range(2):
                 r0 = (i % CHUNKS) * ct + (a * 2 + h) * ht
-                out[r0:r0 + ht, :] = (
+                out_ref[i // CHUNKS, r0:r0 + ht, :] = (
                     up32(q2, e, q, h) + up32(r2f, e, 0, h) + up32(r2f, e, 1, h)
                 ).astype(BF16)
 
@@ -313,9 +336,9 @@
             recv(rzf.at[d, 1 - d], zs.at[2 + d], zr.at[2 + d])
             recv(rzf.at[d, d], zs.at[4 + d], zr.at[4 + d])
         for h in range(2):
-            for m, out in enumerate((gg_ref, ug_ref, dg_ref)):
+            for m in range(3):
                 for e in range(half):
-                    out[0, h * half + e] = (
+                    grad_ref[m, h * half + e] = (
                         up32(gr, z, h, m, e) + up32(rzf, 0, h, m, e) + up32(rzf, 1, h, m, e)
                     )
 
@@ -345,13 +368,13 @@
             e = lax.rem(k, per)
             h = e // half
             e = lax.rem(e, half)
-            xk = x[rows_in[0, k]]
-            bk = gb[cols_in[0, k]]
+            xk = x[lists[0, k]]
+            bk = gb[lists[1, k]]
             g = lax.dot_general(xk, bk, TN, preferred_element_type=F32).astype(BF16)
             gr[d, h, 0, e] = g[:, :blk]
             gr[d, h, 1, e] = g[:, blk:]
-            ak = act[rows_dn[0, k]]
-            ok = og[cols_dn[0, k]]
+            ak = act[lists[2, k]]
+            ok = og[lists[3, k]]
             gr[d, h, 2, e] = lax.dot_general(ak, ok, TN, preferred_element_type=F32).astype(BF16)
             return carry
 
@@ -395,6 +418,13 @@
         c.wait_send()
 
 
+def finish(sums, tile_sums, ffn_ref, ing_ref, gg_ref, ug_ref, dg_ref):
+    ffn_ref[...] = sums[0]
+    ing_ref[...] = sums[1]
+    for m, ref in enumerate((gg_ref, ug_ref, dg_ref)):
+        ref[0] = tile_sums[m]
+
+
 def on_device(
     inputs, out_grad, gate_tiles, up_tiles, down_tiles, in_rows, in_cols, down_rows, down_cols
 ):
@@ -408,29 +438,17 @@
     half = n_tiles // RING // 2
     ev = steps * 2
     any_spec = pl.BlockSpec(memory_space=pl.ANY)
-    smem = pl.BlockSpec(memory_space=pltpu.SMEM)
     vmem = pl.BlockSpec(memory_space=pltpu.VMEM)
     dma = pltpu.SemaphoreType.DMA
-    col_blocks = hidden // blk
-    keys = jnp.concatenate(
-        [in_rows * col_blocks + in_cols, down_rows * row_blocks + down_cols], axis=0
-    )
-    cells = jnp.arange(row_blocks * col_blocks, dtype=jnp.int32)
-    order = jnp.arange(n_tiles, dtype=jnp.int32)
-    inv = n_tiles + jnp.sum(
-        jnp.where(keys[:, :, None] == cells, order[:, None] - n_tiles, 0), axis=1, dtype=jnp.int32
-    )
-    return pl.pallas_call(
+    entries = row_blocks * hidden // blk
+    sums, tile_sums = pl.pallas_call(
         kernel,
         out_shape=(
-            jax.ShapeDtypeStruct((tok, blk), BF16),
-            jax.ShapeDtypeStruct((tok, blk), BF16),
-            jax.ShapeDtypeStruct(gate_tiles.shape, F32),
-            jax.ShapeDtypeStruct(gate_tiles.shape, F32),
-            jax.ShapeDtypeStruct(gate_tiles.shape, F32),
+            jax.ShapeDtypeStruct((2, tok, blk), BF16),
+            jax.ShapeDtypeStruct((3,) + gate_tiles.shape[1:], F32),
         ),
-        in_specs=[any_spec] * 5 + [smem] * 5,
-        out_specs=[vmem] * 5,
+        in_specs=[any_spec] * 9,
+        out_specs=[vmem] * 2,
         scratch_shapes=[
             pltpu.VMEM((row_blocks, tok, blk), BF16),
             pltpu.VMEM((row_blocks, tok, blk), BF16),
@@ -452,7 +470,10 @@
             pltpu.VMEM((RING, 2, 3, half, blk, blk), BF16),
             pltpu.VMEM((2, 3, half, blk, blk), BF16),
             pltpu.VMEM((2, 2, 3, half, blk, blk), BF16),
-            dma((5,)),
+            pltpu.SMEM((4, n_tiles), jnp.int32),
+            pltpu.SMEM((entries,), jnp.int32),
+            pltpu.SMEM((entries,), jnp.int32),
+            dma((9,)),
             dma((3, 4)),
             dma((3, 4)),
             dma((steps, 2)),
@@ -467,8 +488,14 @@
         compiler_params=pltpu.CompilerParams(
             collective_id=0, has_side_effects=True, vmem_limit_bytes=60 * 1024 * 1024
         ),
-    )(inputs, out_grad, gate_tiles, up_tiles, down_tiles, in_rows, in_cols, down_rows, down_cols,
-      inv)
+    )(inputs, out_grad, gate_tiles, up_tiles, down_tiles, in_rows, in_cols, down_rows, down_cols)
+    return pl.pallas_call(
+        finish,
+        out_shape=(jax.ShapeDtypeStruct((tok, blk), BF16),) * 2
+        + (jax.ShapeDtypeStruct(gate_tiles.shape, F32),) * 3,
+        in_specs=[vmem] * 2,
+        out_specs=[vmem] * 5,
+    )(sums, tile_sums)
 
 
 def solution(mesh):

time: 90.5 us -> 82.2 us (0.908)
  local copies, waits for them, and re-layouts: 8.14 us -> 0 us
  Pallas kernels: 79.4 us -> 80.9 us
  other arithmetic: 1.38 us -> 0 us
    unnamed x5 -> x0, local copies, waits for them, and re-layouts: 8.14 us -> none
    pallas_call x1 -> x2, Pallas kernels: 79.4 us -> 80.9 us  [the longest x1 78.7 us: on_device(): pl.pallas_call(kernel, out_shape=(jax.ShapeDtypeStruct((2, tok, blk), BF1...]
    add x2 -> x0, other arithmetic: 1.28 us -> none  [the longest x1 0.71 us: on_device(): down_rows * row_blocks + down_cols]
where the time goes in v1:
time: 82.2 us; the launch traced here: 81.5 us
  Pallas kernels  80.9 us (98%)
    pallas_call x1, Pallas kernels, on_device(): pl.pallas_call(kernel, out_shape=(jax.ShapeDtypeStruct((2, tok, blk), BF1...  78.7 us
    pallas_call x1, Pallas kernels, on_device(): pl.pallas_call(finish, out_shape=(jax.ShapeDtypeStruct((tok, blk), BF16),...  2.19 us

profile of v1, /device:TPU:0, one launch (start us, length us, event | category | flops | bytes accessed | tf_op | source)
XLA Modules:
  0.0 81.5 jit_solution(13954646641371783256)
XLA Ops:
  0.6 78.7 %shard_map.128 = (bf16[2,512,128]{2,1,0:T(8,128)(2,1)}, f32[3,4,128,128]{3,2,1,0:T(8,128)}) custom-call(bf16[512,4096]{1,0:T(8,128)(2,1)} %x_hbm.1, bf16[512,4096]{1,0:T(8,128)(2,1)} %og_hbm.1, bf16[1,4,128,128]{3,2,1,0:T(8,128)(2,1)} %gt_hbm.1, bf16[1,4,128,128]{3,2,1,0:T(8,128)(2,1)} %ut_hbm.1, bf16[1,4,128,128]{3,2,1,0:T(8,128)(2,1)} %dt_hbm.1, ...), custom_call_target="tpu_custom_call" | custom-call | tf_op jit(solution)/shard_map/pallas_call | solution.py:444
  79.3 2.2 %shard_map.129 = (bf16[512,128]{1,0:T(8,128)(2,1)}, bf16[512,128]{1,0:T(8,128)(2,1)}, f32[1,4,128,128]{3,2,1,0:T(8,128)}, f32[1,4,128,128]{3,2,1,0:T(8,128)}, f32[1,4,128,128]{3,2,1,0:T(8,128)}) custom-call(bf16[2,512,128]{2,1,0:T(8,128)(2,1)} %get-tuple-element.7.sums, f32[3,4,128,128]{3,2,1,0:T(8,128)} %get-tuple-element.8.tile_sums), custom_call_target="tpu_custom_call" | custom-call | tf_op jit(solution)/shard_map/pallas_call | solution.py:492

commit v2 on v1

--- a/solution.py
+++ b/solution.py
@@ -190,9 +190,7 @@
 
     lax.fori_loop(0, row_blocks, build_dn, 0)
 
-    def put(i, n, val):
-        yy = n // RING
-        xx = lax.rem(n, RING)
+    def put(i, yy, xx, val):
         for cc in range(2):
             for a, (d1, d2) in enumerate(((xx, yy), (yy, xx))):
                 for h in range(2):
@@ -200,26 +198,27 @@
                     part[i, cc, a, d1, h, d2] = val[r0:r0 + ht, cc * blk:(cc + 1) * blk].astype(BF16)
 
     def out_part(k):
-        def step(n, carry):
-            val = jnp.dot(
-                wide(act, pl.ds(k * ct, ct)), wd[:, pl.ds(n * 2 * blk, 2 * blk)],
-                preferred_element_type=F32,
-            )
-            put(k, n, val)
+        def step(yy, carry):
+            lhs = wide(act, pl.ds(k * ct, ct))
+            for xx in range(RING):
+                cols = pl.ds((yy * RING + xx) * 2 * blk, 2 * blk)
+                put(k, yy, xx, jnp.dot(lhs, wd[:, cols], preferred_element_type=F32))
             return carry
 
-        lax.fori_loop(0, row_blocks // 2, step, 0)
+        lax.fori_loop(0, RING, step, 0)
 
     def in_part(k):
-        def step(n, carry):
-            val = lax.dot_general(
-                wide(gb, pl.ds(k * ct, ct)), wgu[pl.ds(n * 2 * blk, 2 * blk), :], NT,
-                preferred_element_type=F32,
-            )
-            put(CHUNKS + k, n, val)
+        def step(yy, carry):
+            lhs = wide(gb, pl.ds(k * ct, ct))
+            for xx in range(RING):
+                rows = pl.ds((yy * RING + xx) * 2 * blk, 2 * blk)
+                put(
+                    CHUNKS + k, yy, xx,
+                    lax.dot_general(lhs, wgu[rows, :], NT, preferred_element_type=F32),
+                )
             return carry
 
-        lax.fori_loop(0, row_blocks // 2, step, 0)
+        lax.fori_loop(0, RING, step, 0)
 
     def core_send(i):
         for a in range(2):
@@ -389,30 +388,30 @@
     ev_a(1)
     ev_b(0)
     back(1)
-    ev_b(1)
     in_part(0)
     core_send(2)
+    ev_b(1)
     ev_c(0)
+    grads()
+    ev_z0()
+    ev_a(2)
+    ev_d(0)
+    ev_c(1)
     in_part(1)
     core_send(3)
-    ev_a(2)
-    ev_c(1)
-    ev_d(0)
-    grads()
-    ev_z0()
-    ev_a(3)
     ev_b(2)
     ev_e(0)
+    ev_a(3)
     ev_d(1)
+    ev_z1()
     ev_b(3)
     ev_c(2)
-    ev_z1()
     ev_e(1)
+    ev_d(2)
     ev_c(3)
-    ev_d(2)
+    ev_z2()
+    ev_e(2)
     ev_d(3)
-    ev_e(2)
-    ev_z2()
     ev_e(3)
     for c in sends:
         c.wait_send()

time: 82.2 us -> 74.9 us (0.911)
  Pallas kernels: 80.9 us -> 74.1 us
    pallas_call x1, Pallas kernels: 78.7 us -> 71.9 us  [on_device(): pl.pallas_call(kernel, out_shape=(jax.ShapeDtypeStruct((2, tok, blk), BF1...]
where the time goes in v2:
time: 74.9 us; the launch traced here: 74.8 us
  Pallas kernels  74.1 us (99%)
    pallas_call x1, Pallas kernels, on_device(): pl.pallas_call(kernel, out_shape=(jax.ShapeDtypeStruct((2, tok, blk), BF1...  71.9 us
    pallas_call x1, Pallas kernels, on_device(): pl.pallas_call(finish, out_shape=(jax.ShapeDtypeStruct((tok, blk), BF16),...  2.19 us

profile of v2, /device:TPU:0, one launch (start us, length us, event | category | flops | bytes accessed | tf_op | source)
XLA Modules:
  0.0 74.8 jit_solution(9757238957541870397)
XLA Ops:
  0.6 71.9 %shard_map.128 = (bf16[2,512,128]{2,1,0:T(8,128)(2,1)}, f32[3,4,128,128]{3,2,1,0:T(8,128)}) custom-call(bf16[512,4096]{1,0:T(8,128)(2,1)} %x_hbm.1, bf16[512,4096]{1,0:T(8,128)(2,1)} %og_hbm.1, bf16[1,4,128,128]{3,2,1,0:T(8,128)(2,1)} %gt_hbm.1, bf16[1,4,128,128]{3,2,1,0:T(8,128)(2,1)} %ut_hbm.1, bf16[1,4,128,128]{3,2,1,0:T(8,128)(2,1)} %dt_hbm.1, ...), custom_call_target="tpu_custom_call" | custom-call | tf_op jit(solution)/shard_map/pallas_call | solution.py:443
  72.6 2.2 %shard_map.129 = (bf16[512,128]{1,0:T(8,128)(2,1)}, bf16[512,128]{1,0:T(8,128)(2,1)}, f32[1,4,128,128]{3,2,1,0:T(8,128)}, f32[1,4,128,128]{3,2,1,0:T(8,128)}, f32[1,4,128,128]{3,2,1,0:T(8,128)}) custom-call(bf16[2,512,128]{2,1,0:T(8,128)(2,1)} %get-tuple-element.7.sums, f32[3,4,128,128]{3,2,1,0:T(8,128)} %get-tuple-element.8.tile_sums), custom_call_target="tpu_custom_call" | custom-call | tf_op jit(solution)/shard_map/pallas_call | solution.py:491

commit v3 on v1

--- a/solution.py
+++ b/solution.py
@@ -22,7 +22,7 @@
 def kernel(
     x_hbm, og_hbm, gt_hbm, ut_hbm, dt_hbm, rows_in_hbm, cols_in_hbm, rows_dn_hbm, cols_dn_hbm,
     out_ref, grad_ref,
-    x, og, tg, tu, td, wgu, wd, hid, act, gb, part, rc, r1r, r1f, q2, r2r, r2f, gr, rzr, rzf,
+    x, og, tg, tu, td, wgu, wd, hid, act, gb, pp, part, rc, r1r, r1f, q2, r2r, r2f, gr, rzr, rzf,
     lists, inv_in, inv_dn,
     lsem, ags, agr, cs, cr, s1s, s1r, s2s, s2r, zs, zr,
 ):
@@ -80,14 +80,6 @@
     for c in loads:
         c.start()
 
-    def load_block(r, carry):
-        cols = pl.ds(r * blk, blk)
-        pltpu.make_async_copy(x_hbm.at[:, cols], x.at[r], lsem.at[3]).start()
-        pltpu.make_async_copy(og_hbm.at[:, cols], og.at[r], lsem.at[4]).start()
-        return carry
-
-    lax.fori_loop(0, row_blocks, load_block, 0)
-
     lists_hbm = (rows_in_hbm, cols_in_hbm, rows_dn_hbm, cols_dn_hbm)
     list_loads = [
         pltpu.make_async_copy(lists_hbm[j].at[0], lists.at[j], lsem.at[5 + j]) for j in range(4)
@@ -122,8 +114,16 @@
             piece = tiles[m].at[pl.ds(wrap(z + 2) * per + d * half, half)]
             remote(piece, piece, ags.at[m, 2 + d], agr.at[m, 2 + d], partner).wait_recv()
 
-    ag_own(0)
-    ag_own(1)
+    for m in range(3):
+        ag_own(m)
+
+    def load_block(r, carry):
+        cols = pl.ds(r * blk, blk)
+        pltpu.make_async_copy(x_hbm.at[:, cols], x.at[r], lsem.at[3]).start()
+        pltpu.make_async_copy(og_hbm.at[:, cols], og.at[r], lsem.at[4]).start()
+        return carry
+
+    lax.fori_loop(0, row_blocks, load_block, 0)
 
     for c in list_loads:
         c.wait()
@@ -144,109 +144,121 @@
     for m in range(3):
         tiles[m][n_tiles] = jnp.zeros((blk, blk), BF16)
 
-    ag_relay(0)
-    ag_relay(1)
-    ag_own(2)
-    loads[0].wait()
-    loads[1].wait()
-    ag_last(0)
-    ag_last(1)
-
-    def build_gu(r, carry):
-        rows = pl.ds(r * blk, blk)
-        for c in range(col_blocks):
-            i = inv_in[r * col_blocks + c]
-            wgu[rows, 2 * c * blk:(2 * c + 1) * blk] = tg[i]
-            wgu[rows, (2 * c + 1) * blk:(2 * c + 2) * blk] = tu[i]
-        return carry
-
-    lax.fori_loop(0, row_blocks, build_gu, 0)
-    ag_relay(2)
+    for m in range(3):
+        ag_relay(m)
+
+    pairs = row_blocks // 2
+
+    def place(j):
+        return pl.ds((lax.rem(j, 2) * pairs + j // 2) * blk, blk)
+
+    def build_in(m):
+        def step(r, carry):
+            rows = place(r)
+            for c in range(col_blocks):
+                c0 = (2 * c + m) * blk
+                wgu[rows, c0:c0 + blk] = tiles[m][inv_in[r * col_blocks + c]]
+            return carry
+
+        loads[m].wait()
+        ag_last(m)
+        lax.fori_loop(0, row_blocks, step, 0)
+
+    build_in(0)
+    build_in(1)
     pltpu.make_async_copy(x, x, lsem.at[3]).wait()
 
-    def wide(ref, rows):
-        return jnp.concatenate([ref[r, rows] for r in range(ref.shape[0])], axis=1)
-
-    def forward(n, carry):
-        rows = pl.ds((n // col_blocks) * ct, ct)
-        c = lax.rem(n, col_blocks)
-        cols = pl.ds(c * 2 * blk, 2 * blk)
-        h = jnp.dot(wide(x, rows), wgu[:, cols], preferred_element_type=F32)
-        hid[rows, cols] = h
-        gate = h[:, :blk]
-        act[c, rows] = (gate * jax.nn.sigmoid(gate) * h[:, blk:]).astype(BF16)
-        return carry
-
-    lax.fori_loop(0, CHUNKS * col_blocks, forward, 0)
-    loads[2].wait()
-    pltpu.make_async_copy(og, og, lsem.at[4]).wait()
-    ag_last(2)
+    by_core = [2 * i + cc for cc in range(2) for i in range(pairs)]
+
+    def wide(ref, rows, order):
+        return jnp.concatenate([ref[r, rows] for r in order], axis=1)
+
+    def forward(k):
+        rows = pl.ds(k * ct, ct)
+
+        def step(c, carry):
+            cols = pl.ds(c * 2 * blk, 2 * blk)
+            h = jnp.dot(wide(x, rows, by_core), wgu[:, cols], preferred_element_type=F32)
+            hid[rows, cols] = h
+            gate = h[:, :blk]
+            act[c, rows] = (gate * jax.nn.sigmoid(gate) * h[:, blk:]).astype(BF16)
+            return carry
+
+        lax.fori_loop(0, col_blocks, step, 0)
 
     def build_dn(j, carry):
-        cols = pl.ds(j * blk, blk)
+        cols = place(j)
         for c in range(col_blocks):
             wd[c * blk:(c + 1) * blk, cols] = td[inv_dn[c * row_blocks + j]]
         return carry
 
-    lax.fori_loop(0, row_blocks, build_dn, 0)
-
-    def put(i, n, val):
-        yy = n // RING
-        xx = lax.rem(n, RING)
-        for cc in range(2):
-            for a, (d1, d2) in enumerate(((xx, yy), (yy, xx))):
-                for h in range(2):
-                    r0 = (a * 2 + h) * ht
-                    part[i, cc, a, d1, h, d2] = val[r0:r0 + ht, cc * blk:(cc + 1) * blk].astype(BF16)
-
-    def out_part(k):
-        def step(n, carry):
-            val = jnp.dot(
-                wide(act, pl.ds(k * ct, ct)), wd[:, pl.ds(n * 2 * blk, 2 * blk)],
-                preferred_element_type=F32,
-            )
-            put(k, n, val)
-            return carry
-
-        lax.fori_loop(0, row_blocks // 2, step, 0)
-
-    def in_part(k):
-        def step(n, carry):
-            val = lax.dot_general(
-                wide(gb, pl.ds(k * ct, ct)), wgu[pl.ds(n * 2 * blk, 2 * blk), :], NT,
-                preferred_element_type=F32,
-            )
-            put(CHUNKS + k, n, val)
-            return carry
-
-        lax.fori_loop(0, row_blocks // 2, step, 0)
-
-    def core_send(i):
-        for a in range(2):
-            send(part.at[i, 1 - core, a], rc.at[i, a], cs.at[i, a], cr.at[i, a], partner)
+    def down_ready():
+        loads[2].wait()
+        pltpu.make_async_copy(og, og, lsem.at[4]).wait()
+        ag_last(2)
+        lax.fori_loop(0, row_blocks, build_dn, 0)
 
     def recv(ref, ss, rs):
         remote(ref, ref, ss, rs, partner).wait_recv()
 
+    def half_part(i, mine, product):
+        cc = core if mine else 1 - core
+
+        def step(yh, carry):
+            for ye in range(2):
+                yy = yh * 2 + ye
+                for xp in range(2):
+                    val = product(pl.ds((cc * pairs + yy * RING + xp * 2) * blk, 2 * blk))
+                    for xe in range(2):
+                        xx = xp * 2 + xe
+                        for a, (d1, d2) in enumerate(((xx, yy), (yy, xx))):
+                            for h in range(2):
+                                r0 = (a * 2 + h) * ht
+                                v = val[r0:r0 + ht, xe * blk:(xe + 1) * blk]
+                                if mine:
+                                    v = v + rc[i, a, d1, h, d2].astype(F32)
+                                    part[i, a, d1, h, d2] = v.astype(BF16)
+                                else:
+                                    pp[i, a, d1, h, d2] = v.astype(BF16)
+            return carry
+
+        if mine:
+            for a in range(2):
+                recv(rc.at[i, a], cs.at[i, a], cr.at[i, a])
+        lax.fori_loop(0, RING // 2, step, 0)
+        if not mine:
+            for a in range(2):
+                send(pp.at[i, a], rc.at[i, a], cs.at[i, a], cr.at[i, a], partner)
+
+    def out_part(k, mine):
+        lhs = wide(act, pl.ds(k * ct, ct), range(col_blocks))
+        half_part(
+            k, mine, lambda f: jnp.dot(lhs, wd[:, f], preferred_element_type=F32)
+        )
+
+    def in_part(k, mine):
+        lhs = wide(gb, pl.ds(k * ct, ct), range(col_blocks))
+        half_part(
+            CHUNKS + k, mine,
+            lambda f: lax.dot_general(lhs, wgu[f, :], NT, preferred_element_type=F32),
+        )
+
     def ev_a(i):
-        for a in range(2):
-            ax = axes[a][0]
-            p = pos[ax]
-            e = i * 2 + a
-            recv(rc.at[i, a], cs.at[i, a], cr.at[i, a])
-            far = wrap(p + 2)
-            part[i, core, a, far] = (up32(part, i, core, a, far) + up32(rc, i, a, far)).astype(BF16)
-            for d, s in enumerate((1, -1)):
-                send(part.at[i, core, a, far, d], r1r.at[e, d], s1s.at[e, d], s1r.at[e, d], nbr(ax, s))
-            for d, s in enumerate((1, -1)):
-                q = wrap(p + s)
-                h = 1 - d
-                part[i, core, a, q, h] = (
-                    up32(part, i, core, a, q, h) + up32(rc, i, a, q, h)
-                ).astype(BF16)
+        for d, s in enumerate((1, -1)):
+            for a in range(2):
+                ax = axes[a][0]
+                e = i * 2 + a
                 send(
-                    part.at[i, core, a, q, h], r1f.at[e, d, h], s1s.at[e, 2 + d],
-                    s1r.at[e, 2 + d], nbr(ax, s),
+                    part.at[i, a, wrap(pos[ax] + 2), d], r1r.at[e, d], s1s.at[e, d],
+                    s1r.at[e, d], nbr(ax, s),
+                )
+        for d, s in enumerate((1, -1)):
+            for a in range(2):
+                ax = axes[a][0]
+                e = i * 2 + a
+                send(
+                    part.at[i, a, wrap(pos[ax] + s), 1 - d], r1f.at[e, d, 1 - d],
+                    s1s.at[e, 2 + d], s1r.at[e, 2 + d], nbr(ax, s),
                 )
 
     def ev_b(i):
@@ -257,11 +269,9 @@
             for d, s in enumerate((1, -1)):
                 q = wrap(p + s)
                 recv(r1r.at[e, d], s1s.at[e, d], s1r.at[e, d])
-                part[i, core, a, q, d] = (
-                    up32(part, i, core, a, q, d) + up32(rc, i, a, q, d) + up32(r1r, e, d)
-                ).astype(BF16)
+                part[i, a, q, d] = (up32(part, i, a, q, d) + up32(r1r, e, d)).astype(BF16)
                 send(
-                    part.at[i, core, a, q, d], r1f.at[e, d, d], s1s.at[e, 4 + d],
+                    part.at[i, a, q, d], r1f.at[e, d, d], s1s.at[e, 4 + d],
                     s1r.at[e, 4 + d], nbr(ax, s),
                 )
 
@@ -276,8 +286,7 @@
                 recv(r1f.at[e, d, d], s1s.at[e, 4 + d], s1r.at[e, 4 + d])
             for h in range(2):
                 val = (
-                    up32(part, i, core, a, p, h) + up32(rc, i, a, p, h)
-                    + up32(r1f, e, 0, h) + up32(r1f, e, 1, h)
+                    up32(part, i, a, p, h) + up32(r1f, e, 0, h) + up32(r1f, e, 1, h)
                 ).astype(BF16)
                 for d2 in range(RING):
                     q2[e, d2, h] = val[d2]
@@ -319,9 +328,13 @@
 
     def ev_z0():
         far = wrap(z + 2)
+        grads(far)
         for d, s in enumerate((1, -1)):
             send(gr.at[far, d], rzr.at[d], zs.at[d], zr.at[d], nbr("z", s))
+
+    def ev_zp():
         for d, s in enumerate((1, -1)):
+            grads(wrap(z + s))
             send(gr.at[wrap(z + s), 1 - d], rzf.at[d, 1 - d], zs.at[2 + d], zr.at[2 + d], nbr("z", s))
 
     def ev_z1():
@@ -347,7 +360,7 @@
 
         def step(n, carry):
             ag = lax.dot_general(
-                wide(og, rows), wd[pl.ds(n * 2 * blk, 2 * blk), :], NT, preferred_element_type=F32
+                wide(og, rows, by_core), wd[pl.ds(n * 2 * blk, 2 * blk), :], NT, preferred_element_type=F32
             )
             for e in range(2):
                 c = n * 2 + e
@@ -362,57 +375,56 @@
 
         lax.fori_loop(0, col_blocks // 2, step, 0)
 
-    def grads():
-        def step(k, carry):
-            d = k // per
-            e = lax.rem(k, per)
-            h = e // half
-            e = lax.rem(e, half)
-            xk = x[lists[0, k]]
-            bk = gb[lists[1, k]]
-            g = lax.dot_general(xk, bk, TN, preferred_element_type=F32).astype(BF16)
+    def grads(d):
+        for j in range(per):
+            k = d * per + j
+            h, e = j // half, j % half
+            g = lax.dot_general(
+                x[lists[0, k]], gb[lists[1, k]], TN, preferred_element_type=F32
+            ).astype(BF16)
             gr[d, h, 0, e] = g[:, :blk]
             gr[d, h, 1, e] = g[:, blk:]
-            ak = act[lists[2, k]]
-            ok = og[lists[3, k]]
-            gr[d, h, 2, e] = lax.dot_general(ak, ok, TN, preferred_element_type=F32).astype(BF16)
-            return carry
-
-        lax.fori_loop(0, n_tiles, step, 0)
-
-    out_part(0)
-    core_send(0)
-    out_part(1)
-    core_send(1)
+            gr[d, h, 2, e] = lax.dot_general(
+                act[lists[2, k]], og[lists[3, k]], TN, preferred_element_type=F32
+            ).astype(BF16)
+
+    forward(0)
+    down_ready()
+    out_part(0, False)
+    forward(1)
+    out_part(1, False)
+    out_part(0, True)
     ev_a(0)
     back(0)
+    out_part(1, True)
     ev_a(1)
+    in_part(0, False)
     ev_b(0)
     back(1)
+    in_part(0, True)
+    ev_a(2)
+    in_part(1, False)
     ev_b(1)
-    in_part(0)
-    core_send(2)
+    ev_z0()
     ev_c(0)
-    in_part(1)
-    core_send(3)
-    ev_a(2)
+    in_part(1, True)
+    ev_a(3)
+    ev_zp()
+    ev_b(2)
     ev_c(1)
     ev_d(0)
-    grads()
-    ev_z0()
-    ev_a(3)
-    ev_b(2)
+    grads(z)
+    ev_b(3)
+    ev_z1()
+    ev_d(1)
+    ev_c(2)
     ev_e(0)
-    ev_d(1)
-    ev_b(3)
-    ev_c(2)
-    ev_z1()
+    ev_c(3)
     ev_e(1)
-    ev_c(3)
     ev_d(2)
+    ev_z2()
     ev_d(3)
     ev_e(2)
-    ev_z2()
     ev_e(3)
     for c in sends:
         c.wait_send()
@@ -460,7 +472,8 @@
             pltpu.VMEM((tok, 2 * hidden), F32),
             pltpu.VMEM((hidden // blk, tok, blk), BF16),
             pltpu.VMEM((hidden // blk, tok, 2 * blk), BF16),
-            pltpu.VMEM((steps, 2, 2, RING, 2, RING, ht, blk), BF16),
+            pltpu.VMEM((steps, 2, RING, 2, RING, ht, blk), BF16),
+            pltpu.VMEM((steps, 2, RING, 2, RING, ht, blk), BF16),
             pltpu.VMEM((steps, 2, RING, 2, RING, ht, blk), BF16),
             pltpu.VMEM((ev, 2, RING, ht, blk), BF16),
             pltpu.VMEM((ev, 2, 2, RING, ht, blk), BF16),

time: 82.2 us -> 69 us (0.84)
  Pallas kernels: 80.9 us -> 68.2 us
    pallas_call x1, Pallas kernels: 78.7 us -> 66 us  [on_device(): pl.pallas_call(kernel, out_shape=(jax.ShapeDtypeStruct((2, tok, blk), BF1...]
where the time goes in v3:
time: 69 us; the launch traced here: 68.8 us
  Pallas kernels  68.2 us (99%)
    pallas_call x1, Pallas kernels, on_device(): pl.pallas_call(kernel, out_shape=(jax.ShapeDtypeStruct((2, tok, blk), BF1...  66 us
    pallas_call x1, Pallas kernels, on_device(): pl.pallas_call(finish, out_shape=(jax.ShapeDtypeStruct((tok, blk), BF16),...  2.19 us

profile of v3, /device:TPU:0, one launch (start us, length us, event | category | flops | bytes accessed | tf_op | source)
XLA Modules:
  0.0 68.8 jit_solution(5029615755656863131)
XLA Ops:
  0.6 66.0 %shard_map.128 = (bf16[2,512,128]{2,1,0:T(8,128)(2,1)}, f32[3,4,128,128]{3,2,1,0:T(8,128)}) custom-call(bf16[512,4096]{1,0:T(8,128)(2,1)} %x_hbm.1, bf16[512,4096]{1,0:T(8,128)(2,1)} %og_hbm.1, bf16[1,4,128,128]{3,2,1,0:T(8,128)(2,1)} %gt_hbm.1, bf16[1,4,128,128]{3,2,1,0:T(8,128)(2,1)} %ut_hbm.1, bf16[1,4,128,128]{3,2,1,0:T(8,128)(2,1)} %dt_hbm.1, ...), custom_call_target="tpu_custom_call" | custom-call | tf_op jit(solution)/shard_map/pallas_call | solution.py:456
  66.7 2.2 %shard_map.129 = (bf16[512,128]{1,0:T(8,128)(2,1)}, bf16[512,128]{1,0:T(8,128)(2,1)}, f32[1,4,128,128]{3,2,1,0:T(8,128)}, f32[1,4,128,128]{3,2,1,0:T(8,128)}, f32[1,4,128,128]{3,2,1,0:T(8,128)}) custom-call(bf16[2,512,128]{2,1,0:T(8,128)(2,1)} %get-tuple-element.7.sums, f32[3,4,128,128]{3,2,1,0:T(8,128)} %get-tuple-element.8.tile_sums), custom_call_target="tpu_custom_call" | custom-call | tf_op jit(solution)/shard_map/pallas_call | solution.py:505
